TPU v7x, 128 devices: a whole 4x4x4 slice. The times are simulated.
128 devices in a mesh: gx: 8 (over z, core), gy: 4 (over x), gz: 4 (over y).
Axes of the slice: x: 4, y: 4, z: 4, core: 2. Of those that a mesh axis runs over, the one named last changes fastest.
Arguments:
- snapshots: float32 [16, 128, 128, 1024], P(None, 'gx', 'gy', 'gz'), as said below
- diffusivity: float32 [128, 128, 1024], P('gx', 'gy', 'gz'), may hold values from 0.02 to 0.16
Outputs:
- shifted: float32 [16, 128, 128, 1024], P(None, 'gx', 'gy', 'gz')
- reduced: float32 [16, 16], replicated
- sigmas: float32 [16], replicated
Inputs may be any that keep to these rules, and one draw needn't show every extreme that they name: `snapshots`: real values.
All inputs are finite; a program needn't handle non-finite values.
Results may differ from a plain program's by a relative error of at most 0.0003.
Values sent between devices are 32-bit elements; how exact they have to be, the bound alone decides.
A program may use at most 128 MiB of HBM per device.

v0:
```python
import jax
import jax.numpy as jnp
import numpy as np
from jax import lax
from jax.sharding import PartitionSpec as P

SNAPS = 16
RANK = 12
SWEEPS = 6


def extended(block, sides, width):
    for axis, dim in sides:
        count = lax.axis_size(axis)
        forward = [(i, i + 1) for i in range(count - 1)]
        forward.append((count - 1, 0))
        backward = [(target, source) for source, target in forward]
        low = lax.ppermute(
            lax.slice_in_dim(block, block.shape[dim] - width, None, axis=dim), axis, forward
        )
        high = lax.ppermute(lax.slice_in_dim(block, 0, width, axis=dim), axis, backward)
        block = jnp.concatenate([low, block, high], axis=dim)
    return block


def round_pairs(count):
    players = list(range(count))
    firsts = []
    seconds = []
    for turn in range(count - 1):
        firsts.append([players[i] for i in range(count // 2)])
        seconds.append([players[count - 1 - i] for i in range(count // 2)])
        players = [players[0]] + [players[-1]] + players[1:-1]
    return (np.array(firsts, dtype=np.int32), np.array(seconds, dtype=np.int32))


def jacobi_eigen(small):
    count = small.shape[0]
    first_np, second_np = round_pairs(count)
    firsts = jnp.asarray(first_np)
    seconds = jnp.asarray(second_np)
    eye = jnp.eye(count, dtype=jnp.float32)
    high = lax.Precision.HIGHEST

    def turn(step, carry):
        mat, vecs = carry
        row = step % (count - 1)
        pidx = firsts[row]
        qidx = seconds[row]
        app = mat[pidx, pidx]
        aqq = mat[qidx, qidx]
        apq = mat[pidx, qidx]
        tau = aqq - app
        sgn = jnp.where(tau >= 0, 1.0, -1.0).astype(jnp.float32)
        denom = jnp.abs(tau) + jnp.sqrt(tau * tau + 4.0 * apq * apq)
        tangent = jnp.where(denom > 0, 2.0 * apq * sgn / jnp.where(denom > 0, denom, 1.0), 0.0)
        cosine = 1.0 / jnp.sqrt(1.0 + tangent * tangent)
        sine = tangent * cosine
        onep = jax.nn.one_hot(pidx, count, dtype=jnp.float32)
        oneq = jax.nn.one_hot(qidx, count, dtype=jnp.float32)
        rot = eye + jnp.dot(onep.T, (cosine - 1.0)[:, None] * onep, precision=high)
        rot = rot + jnp.dot(oneq.T, (cosine - 1.0)[:, None] * oneq, precision=high)
        rot = rot + jnp.dot(onep.T, sine[:, None] * oneq, precision=high)
        rot = rot - jnp.dot(oneq.T, sine[:, None] * onep, precision=high)
        mat = jnp.dot(jnp.dot(rot.T, mat, precision=high), rot, precision=high)
        vecs = jnp.dot(vecs, rot, precision=high)
        return (mat, vecs)

    mat, vecs = lax.fori_loop(0, SWEEPS * (count - 1), turn, (small, eye))
    return (jnp.diagonal(mat), vecs)


def factor_pair(gram, cross):
    lower = jnp.linalg.cholesky(gram)
    proj = lax.linalg.triangular_solve(lower, cross, left_side=True, lower=True)
    return (lower.T, proj)


def finish(upper, proj, ncell):
    high = lax.Precision.HIGHEST
    small = jnp.dot(upper, upper.T, precision=high) / ncell
    lam, vecs = jacobi_eigen(small)
    ordered = jnp.sort(lam)[::-1]
    sigmas = jnp.sqrt(ordered)
    keep = (lam >= ordered[RANK - 1]).astype(jnp.float32)
    projector = jnp.dot(vecs * keep[None, :], vecs.T, precision=high)
    inverse = jnp.dot(vecs * (keep / lam)[None, :], vecs.T, precision=high) / ncell
    reduced = jnp.dot(jnp.dot(projector, proj, precision=high), upper.T, precision=high)
    reduced = jnp.dot(reduced, inverse, precision=high)
    return (reduced, sigmas)


def view(padded, dim, offset):
    leading = tuple((slice(None) for lead_pos in range(padded.ndim - 3)))
    parts = [slice(2, padded.shape[padded.ndim - 3 + axis_pos] - 2) for axis_pos in range(3)]
    length = padded.shape[padded.ndim - 3 + dim] - 4
    parts[dim] = slice(2 + offset, 2 + offset + length)
    return padded[leading + tuple(parts)]


def advance(padded, diffusivity):
    field = view(padded, 0, 0)
    lap = -6.0 * field
    for dim in range(3):
        lap = lap + view(padded, dim, 1) + view(padded, dim, -1)

    def slope(dim):
        return (
            8.0 * (view(padded, dim, 1) - view(padded, dim, -1))
            - (view(padded, dim, 2) - view(padded, dim, -2))
        ) / 12.0

    return (
        field
        + diffusivity * lap
        - (0.3 + 0.02 * field) * slope(2)
        - 0.2 * slope(0)
        - 0.15 * slope(1)
    )


def shards(snapshots, diffusivity):
    high = lax.Precision.HIGHEST

    def one_field(index, collected):
        field = lax.dynamic_index_in_dim(snapshots, index, 0, keepdims=False)
        padded = extended(field, (("gx", 0), ("gy", 1), ("gz", 2)), 2)
        return lax.dynamic_update_index_in_dim(collected, advance(padded, diffusivity), index, 0)

    shifted = lax.fori_loop(0, snapshots.shape[0], one_field, jnp.zeros_like(snapshots))
    flat_x = snapshots.reshape(SNAPS, -1)
    flat_y = shifted.reshape(SNAPS, -1)
    gram = jnp.dot(flat_x, flat_x.T, precision=high)
    cross = jnp.dot(flat_x, flat_y.T, precision=high)
    ncell = float(flat_x.shape[1] * lax.axis_size("gx") * lax.axis_size("gy") * lax.axis_size("gz"))
    gram, cross = lax.psum((gram, cross), ("gx", "gy", "gz"))
    upper, proj = factor_pair(gram, cross)
    reduced, sigmas = finish(upper, proj, ncell)
    return (shifted, reduced, sigmas)


def solution(mesh):
    placed = (P(None, "gx", "gy", "gz"), P("gx", "gy", "gz"))
    return jax.shard_map(
        shards,
        mesh=mesh,
        in_specs=placed,
        out_specs=(P(None, "gx", "gy", "gz"), P(), P()),
        check_vma=False,
    )
```

profile of v0, /device:TPU:1, one launch (start us, length us, event | category | flops | bytes accessed | tf_op | source)
XLA Modules:
  0.0 981.1 jit_solution(14451856743499966787)
XLA Ops:
  0.6 407.2 %while.34 = (s32[]{:T(128)}, f32[16,16,32,256]{3,2,1,0:T(8,128)}, f32[16,16,32,256]{3,2,1,0:T(8,128)}, f32[16,32,256]{2,1,0:T(8,128)}, s32[]{:T(128)}, /*index=5*/s32[]{:T(128)}, s32[]{}) while((s32[]{:T(128)}, f32[16,16,32,256]{3,2,1,0:T(8,128)}, f32[16,16,32,256]{3,2,1,0:T(8,128)}, f32[16,32,256]{2,1,0:T(8,128)}, s32[]{:T(128)}, ...), condition=%wide.region_1.2_spmd, body=%wide.region_0.1_spmd.sunk | while | flops 8900611 | bytes 10468449 | solution.py:130
  7.3 2.5 collective-permute-start.2
  11.0 3.0 collective-permute-done.3
  17.2 5.1 collective-permute-done.4
  22.4 3.8 fusion.118
  27.0 7.0 collective-permute-start
  43.8 5.2 collective-permute-done.4
  49.0 3.8 fusion.118
  53.6 6.8 collective-permute-start
  67.3 2.0 collective-permute-start.5
  69.5 5.1 collective-permute-done.4
  74.6 3.8 fusion.118
  79.2 6.3 collective-permute-start
  93.8 1.8 collective-permute-start.5
  95.7 6.0 collective-permute-done.4
  101.7 3.8 fusion.118
  106.3 4.2 collective-permute-start
  121.5 6.5 collective-permute-done.4
  128.0 3.8 fusion.118
  132.6 3.7 collective-permute-start
  145.0 1.8 collective-permute-start.5
  146.9 6.2 collective-permute-done.4
  153.2 3.8 fusion.118
  157.8 4.0 collective-permute-start
  170.2 1.8 collective-permute-start.5
  172.2 6.1 collective-permute-done.4
  178.3 3.8 fusion.118
  182.9 4.1 collective-permute-start
  194.4 1.8 collective-permute-start.5
  196.3 5.1 collective-permute-done.4
  201.4 3.8 fusion.118
  206.1 5.8 collective-permute-start
  220.4 1.8 collective-permute-start.5
  222.3 6.2 collective-permute-done.4
  228.5 3.8 fusion.118
  233.1 4.0 collective-permute-start
  248.1 6.5 collective-permute-done.4
  254.6 3.8 fusion.118
  259.2 3.7 collective-permute-start
  273.4 6.1 collective-permute-done.4
  279.5 3.8 fusion.118
  284.1 4.1 collective-permute-start
  295.8 1.8 collective-permute-start.5
  297.8 5.1 collective-permute-done.4
  302.9 3.8 fusion.118
  307.6 5.5 collective-permute-start
  321.5 1.8 collective-permute-start.5
  323.5 6.0 collective-permute-done.4
  329.5 3.8 fusion.118
  334.2 4.2 collective-permute-start
  347.3 1.8 collective-permute-start.5
  349.2 6.5 collective-permute-done.4
  355.8 3.8 fusion.118
  360.4 3.7 collective-permute-start
  374.6 6.1 collective-permute-done.4
  380.7 3.8 fusion.118
  385.3 4.1 collective-permute-start
  396.9 1.8 collective-permute-start.5
  398.9 5.1 collective-permute-done.4
  404.0 3.8 fusion.118
  407.8 25.4 %fusion.56 = f32[16,16]{0,1:T(8,128)S(1)} fusion(f32[16,16,32,256]{3,2,1,0:T(8,128)} %get-tuple-element.458, f32[16,16,32,256]{3,2,1,0:T(8,128)} %get-tuple-element.270), kind=kOutput, calls=%fused_computation.108 | convolution fusion | flops 402653184 | bytes 16778240 | tf_op jit(solution)/shard_map/dot_general | solution.py:134
  433.2 14.0 %fusion.53 = f32[16,16]{0,1:T(8,128)S(1)} fusion(f32[16,16,32,256]{3,2,1,0:T(8,128)S(1)} %copy-done), kind=kOutput, calls=%fused_computation.105 | convolution fusion | flops 402653184 | bytes 8389632 | tf_op jit(solution)/shard_map/dot_general | solution.py:133
  447.2 69.8 %all-reduce = (f32[16,16]{0,1:T(8,128)S(1)}, f32[16,16]{0,1:T(8,128)S(1)}) all-reduce(f32[16,16]{0,1:T(8,128)S(1)} %fusion.53, f32[16,16]{0,1:T(8,128)S(1)} %fusion.56), channel_id=1, replica_groups=mesh['gx'=8,'gy'=4,'gz'=4] {'gx','gy','gz'}, use_global_device_ids=true, to_apply=%region_2.3 | all-reduce | flops 512 | bytes 4096 | tf_op jit(solution)/shard_map/psum | solution.py:136
  520.2 452.1 %while.35 = (s32[]{:T(128)}, f32[16,16]{1,0:T(8,128)S(1)}, f32[16,16]{0,1:T(8,128)S(1)}, s32[]{:T(128)}, s32[15,8]{1,0:T(8,128)}, /*index=5*/s32[]{:T(128)}, s32[]{:T(128)}, s32[15,8]{1,0:T(8,128)}) while((s32[]{:T(128)}, f32[16,16]{1,0:T(8,128)S(1)}, f32[16,16]{0,1:T(8,128)S(1)}, s32[]{:T(128)}, ...), condition=%wide.region_6.7_spmd.clone.clone, body=%wide.region_5.6_spmd.sunk.clone.clone.sunk | while | flops 249131 | bytes 19833 | solution.py:69
  (1623 shorter events, 620.6 us)
Async XLA Ops:
  1.5 5.0 collective-permute-start
  2.9 4.3 collective-permute-start.1
  9.9 4.1 collective-permute-start.3
  14.2 8.1 collective-permute-start.4
  15.6 6.8 collective-permute-start.5
  27.0 8.1 collective-permute-start
  36.5 4.1 collective-permute-start.3
  40.9 8.1 collective-permute-start.4
  41.9 7.0 collective-permute-start.5
  53.6 7.9 collective-permute-start
  61.8 4.1 collective-permute-start.3
  66.3 8.3 collective-permute-start.4
  67.3 7.3 collective-permute-start.5
  79.2 8.9 collective-permute-start
  88.3 4.1 collective-permute-start.3
  92.7 9.0 collective-permute-start.4
  93.8 7.9 collective-permute-start.5
  106.3 7.5 collective-permute-start
  114.0 4.1 collective-permute-start.3
  118.4 9.6 collective-permute-start.4
  119.5 8.5 collective-permute-start.5
  132.6 6.7 collective-permute-start
  139.5 4.1 collective-permute-start.3
  143.9 9.3 collective-permute-start.4
  145.0 8.2 collective-permute-start.5
  157.8 6.7 collective-permute-start
  164.8 4.1 collective-permute-start.3
  169.2 9.1 collective-permute-start.4
  170.2 8.0 collective-permute-start.5
  182.9 5.8 collective-permute-start
  188.9 4.1 collective-permute-start.3
  193.3 8.2 collective-permute-start.4
  194.4 7.1 collective-permute-start.5
  206.1 8.7 collective-permute-start
  214.8 4.1 collective-permute-start.3
  219.3 9.2 collective-permute-start.4
  220.4 8.1 collective-permute-start.5
  233.1 7.4 collective-permute-start
  240.6 4.1 collective-permute-start.3
  245.0 9.6 collective-permute-start.4
  246.1 8.5 collective-permute-start.5
  259.2 6.6 collective-permute-start
  266.0 4.1 collective-permute-start.3
  270.3 9.2 collective-permute-start.4
  271.4 8.1 collective-permute-start.5
  284.1 6.2 collective-permute-start
  290.4 4.1 collective-permute-start.3
  294.8 8.1 collective-permute-start.4
  295.8 7.1 collective-permute-start.5
  307.6 8.3 collective-permute-start
  316.0 4.1 collective-permute-start.3
  320.5 9.1 collective-permute-start.4
  321.5 8.0 collective-permute-start.5
  334.2 7.5 collective-permute-start
  341.8 4.1 collective-permute-start.3
  346.2 9.6 collective-permute-start.4
  347.3 8.5 collective-permute-start.5
  360.4 6.6 collective-permute-start
  371.5 9.2 collective-permute-start.4
  372.6 8.1 collective-permute-start.5
  385.3 6.1 collective-permute-start
  391.5 4.1 collective-permute-start.3
  396.0 8.1 collective-permute-start.4
  396.9 7.1 collective-permute-start.5
  (33 other events, 116.5 us)
where the time goes:
time: 993 us; the launch traced here: 981 us
  local copies, waits for them, and re-layouts  275 us (28%)
  matrix products  186 us (19%)
  starting transfers between devices  157 us (16%)
  waiting for transfers between devices  151 us (15%)
  other arithmetic  139 us (14%)
  blocking collectives  69.8 us (7%)
    ppermute x48, waiting for transfers between devices, extended(): lax.ppermute(lax.slice_in_dim(block, block.shape[dim] - width, None, axis...  117 us
    ppermute x48, starting transfers between devices, extended(): lax.ppermute(lax.slice_in_dim(block, 0, width, axis=dim), axis, backward)  106 us
    psum x1, blocking collectives, shards(): gram, cross = lax.psum((gram, cross), ('gx', 'gy', 'gz'))  69.8 us
    concatenate x90, other arithmetic, turn(): app = mat[pidx, pidx]  65.6 us
    eq x90, local copies, waits for them, and re-layouts, turn(): onep = jax.nn.one_hot(pidx, count, dtype=jnp.float32)  64.9 us
    dynamic_update_slice x16, other arithmetic, one_field(): lax.dynamic_update_index_in_dim(collected, advance(padded, diffusivity),...  60 us
    gather x90, local copies, waits for them, and re-layouts, turn(): aqq = mat[qidx, qidx]  58.1 us
    gather x90, local copies, waits for them, and re-layouts, turn(): app = mat[pidx, pidx]  58.1 us
  transfers between devices with their start and end apart: 96, of which 65 were waited for; matrix products, arithmetic and copies ran while one was open for 2% of the time, Pallas kernels for 0%

commit v1 on v0

--- a/solution.py
+++ b/solution.py
@@ -133,7 +133,7 @@
     gram = jnp.dot(flat_x, flat_x.T, precision=high)
     cross = jnp.dot(flat_x, flat_y.T, precision=high)
     ncell = float(flat_x.shape[1] * lax.axis_size("gx") * lax.axis_size("gy") * lax.axis_size("gz"))
-    gram, cross = lax.psum((gram, cross), ("gx", "gy", "gz"))
+    gram, cross = lax.psum(lax.psum((gram, cross), "gx"), ("gy", "gz"))
     upper, proj = factor_pair(gram, cross)
     reduced, sigmas = finish(upper, proj, ncell)
     return (shifted, reduced, sigmas)

time: 993 us -> 1020 us (1.027)
  the two profiles are of different devices: /device:TPU:1 before, /device:TPU:0 now
where the time goes in v1:
time: 1020 us; the launch traced here: 1010 us
  local copies, waits for them, and re-layouts  275 us (27%)
  waiting for transfers between devices  213 us (21%)
  matrix products  186 us (18%)
  other arithmetic  139 us (14%)
  starting transfers between devices  99.3 us (10%)
  blocking collectives  95.8 us (9%)
    ppermute x48, waiting for transfers between devices, extended(): lax.ppermute(lax.slice_in_dim(block, block.shape[dim] - width, None, axis...  175 us
    psum x2, blocking collectives, shards(): gram, cross = lax.psum(lax.psum((gram, cross), 'gx'), ('gy', 'gz'))  95.8 us
    concatenate x90, other arithmetic, turn(): app = mat[pidx, pidx]  65.6 us
    eq x90, local copies, waits for them, and re-layouts, turn(): onep = jax.nn.one_hot(pidx, count, dtype=jnp.float32)  64.9 us
    dynamic_update_slice x16, other arithmetic, one_field(): lax.dynamic_update_index_in_dim(collected, advance(padded, diffusivity),...  60 us
    gather x90, local copies, waits for them, and re-layouts, turn(): aqq = mat[qidx, qidx]  58.1 us
    gather x90, local copies, waits for them, and re-layouts, turn(): app = mat[pidx, pidx]  58.1 us
    gather x90, local copies, waits for them, and re-layouts, turn(): apq = mat[pidx, qidx]  57.4 us
  transfers between devices with their start and end apart: 96, of which 84 were waited for; matrix products, arithmetic and copies ran while one was open for 2% of the time, Pallas kernels for 0%

profile of v1, /device:TPU:0, one launch (start us, length us, event | category | flops | bytes accessed | tf_op | source)
XLA Modules:
  0.0 1011.3 jit_solution(516598037169186359)
XLA Ops:
  0.6 411.3 %while.34 = (s32[]{:T(128)}, f32[16,16,32,256]{3,2,1,0:T(8,128)}, f32[16,16,32,256]{3,2,1,0:T(8,128)}, f32[16,32,256]{2,1,0:T(8,128)}, s32[]{:T(128)}, /*index=5*/s32[]{:T(128)}, s32[]{}) while((s32[]{:T(128)}, f32[16,16,32,256]{3,2,1,0:T(8,128)}, f32[16,16,32,256]{3,2,1,0:T(8,128)}, f32[16,32,256]{2,1,0:T(8,128)}, s32[]{:T(128)}, ...), condition=%wide.region_1.2_spmd, body=%wide.region_0.1_spmd.sunk | while | flops 8900611 | bytes 10468449 | solution.py:130
  1.5 3.6 collective-permute-start
  7.0 3.0 collective-permute-done.1
  10.1 2.8 collective-permute-start.2
  14.6 3.5 collective-permute-done.3
  21.8 5.8 collective-permute-done.4
  28.0 3.8 fusion.118
  35.8 3.0 collective-permute-done.1
  41.0 2.0 collective-permute-done.2
  46.4 2.0 collective-permute-start.5
  48.5 5.8 collective-permute-done.4
  54.4 3.8 fusion.118
  61.1 3.0 collective-permute-done.1
  71.0 2.6 collective-permute-start.5
  73.7 5.8 collective-permute-done.4
  79.5 3.8 fusion.118
  86.0 3.0 collective-permute-done.1
  89.2 2.0 collective-permute-start.3
  96.0 2.1 collective-permute-start.5
  98.2 6.3 collective-permute-done.4
  104.5 3.8 fusion.118
  111.1 3.0 collective-permute-done.1
  123.4 6.9 collective-permute-done.4
  130.3 3.8 fusion.118
  136.8 3.0 collective-permute-done.1
  149.1 6.6 collective-permute-done.4
  155.7 3.8 fusion.118
  162.3 3.0 collective-permute-done.1
  174.6 6.4 collective-permute-done.4
  181.0 3.8 fusion.118
  187.6 3.0 collective-permute-done.1
  200.0 5.8 collective-permute-done.4
  205.9 3.8 fusion.118
  212.4 3.0 collective-permute-done.1
  224.6 6.5 collective-permute-done.4
  231.1 3.8 fusion.118
  237.7 3.0 collective-permute-done.1
  242.8 2.0 collective-permute-done.2
  250.0 6.9 collective-permute-done.4
  256.9 3.8 fusion.118
  263.4 3.0 collective-permute-done.1
  275.7 6.5 collective-permute-done.4
  282.2 3.8 fusion.118
  288.8 3.0 collective-permute-done.1
  293.9 2.0 collective-permute-done.2
  301.1 5.8 collective-permute-done.4
  307.0 3.8 fusion.118
  313.6 3.0 collective-permute-done.1
  325.9 6.4 collective-permute-done.4
  332.3 3.8 fusion.118
  338.9 3.0 collective-permute-done.1
  351.1 6.9 collective-permute-done.4
  358.1 3.8 fusion.118
  364.6 3.0 collective-permute-done.1
  376.9 6.5 collective-permute-done.4
  383.4 3.8 fusion.118
  390.0 3.0 collective-permute-done.1
  402.3 5.8 collective-permute-done.4
  408.2 3.8 fusion.118
  411.9 25.4 %fusion.56 = f32[16,16]{0,1:T(8,128)S(1)} fusion(f32[16,16,32,256]{3,2,1,0:T(8,128)} %get-tuple-element.460, f32[16,16,32,256]{3,2,1,0:T(8,128)} %get-tuple-element.270), kind=kOutput, calls=%fused_computation.108 | convolution fusion | flops 402653184 | bytes 16778240 | tf_op jit(solution)/shard_map/dot_general | solution.py:134
  437.4 14.0 %fusion.53 = f32[16,16]{0,1:T(8,128)S(1)} fusion(f32[16,16,32,256]{3,2,1,0:T(8,128)S(1)} %copy-done), kind=kOutput, calls=%fused_computation.105 | convolution fusion | flops 402653184 | bytes 8389632 | tf_op jit(solution)/shard_map/dot_general | solution.py:133
  451.4 23.6 %all-reduce.1 = (f32[16,16]{0,1:T(8,128)S(1)}, f32[16,16]{0,1:T(8,128)S(1)}) all-reduce(f32[16,16]{0,1:T(8,128)S(1)} %fusion.53, f32[16,16]{0,1:T(8,128)S(1)} %fusion.56), channel_id=1, replica_groups=mesh['gx'=8,'gy'=4,'gz'=4] {'gx'}, use_global_device_ids=true, to_apply=%region_2.3 | all-reduce | flops 512 | bytes 4096 | tf_op jit(solution)/shard_map/psum | solution.py:136
  475.0 72.3 %all-reduce = (f32[16,16]{0,1:T(8,128)S(1)}, f32[16,16]{0,1:T(8,128)S(1)}) all-reduce(f32[16,16]{0,1:T(8,128)S(1)} %get-tuple-element.324, f32[16,16]{0,1:T(8,128)S(1)} %get-tuple-element.325), channel_id=1, replica_groups=mesh['gx'=8,'gy'=4,'gz'=4] {'gy','gz'}, use_global_device_ids=true, to_apply=%region_3.4 | all-reduce | flops 512 | bytes 4096 | tf_op jit(solution)/shard_map/psum | solution.py:136
  550.4 452.1 %while.35 = (s32[]{:T(128)}, f32[16,16]{1,0:T(8,128)S(1)}, f32[16,16]{0,1:T(8,128)S(1)}, s32[]{:T(128)}, s32[15,8]{1,0:T(8,128)}, /*index=5*/s32[]{:T(128)}, s32[]{:T(128)}, s32[15,8]{1,0:T(8,128)}) while((s32[]{:T(128)}, f32[16,16]{1,0:T(8,128)S(1)}, f32[16,16]{0,1:T(8,128)S(1)}, s32[]{:T(128)}, ...), condition=%wide.region_7.8_spmd.clone.clone, body=%wide.region_6.7_spmd.sunk.clone.clone.sunk | while | flops 249131 | bytes 19833 | solution.py:69
  (1624 shorter events, 639.3 us)
Async XLA Ops:
  1.5 5.5 collective-permute-start
  5.1 4.9 collective-permute-start.1
  12.9 5.2 collective-permute-start.3
  18.4 9.2 collective-permute-start.4
  20.0 8.0 collective-permute-start.5
  39.6 5.2 collective-permute-start.3
  45.1 9.2 collective-permute-start.4
  46.4 8.0 collective-permute-start.5
  59.2 4.9 collective-permute-start.1
  64.7 5.2 collective-permute-start.3
  70.2 9.2 collective-permute-start.4
  71.0 8.5 collective-permute-start.5
  84.1 4.9 collective-permute-start.1
  89.2 5.3 collective-permute-start.3
  94.7 9.8 collective-permute-start.4
  96.0 8.6 collective-permute-start.5
  109.2 4.9 collective-permute-start.1
  114.4 5.2 collective-permute-start.3
  119.9 10.4 %collective-permute-start.4 = (f32[20,36,2]{2,1,0:T(8,128)S(1)}, f32[20,36,2]{2,1,0:T(8,128)S(1)}, u32[]{:S(2)}, u32[]{:S(2)}) collective-permute-start(f32[20,36,2]{2,1,0:T(8,128)S(1)} %get-tuple-element.403), channel_id=1, source_target_pairs={{0,1},{1,2},{2,3},{3,0},{4,5},{5,6},{6,7},{7,4},{8,9},{9,10},{10,1... | collective-permute-start | bytes 17288 | tf_op jit(solution)/shard_map/while/body/eval_jaxpr/ppermute | solution.py:18
  121.3 9.0 collective-permute-start.5
  134.9 4.9 collective-permute-start.1
  140.2 5.2 collective-permute-start.3
  145.7 10.1 collective-permute-start.4
  147.0 8.7 collective-permute-start.5
  160.4 4.9 collective-permute-start.1
  165.6 5.2 collective-permute-start.3
  171.1 9.9 collective-permute-start.4
  172.5 8.5 collective-permute-start.5
  185.7 4.9 collective-permute-start.1
  191.1 5.2 collective-permute-start.3
  196.6 9.2 collective-permute-start.4
  197.9 8.0 collective-permute-start.5
  210.5 4.9 collective-permute-start.1
  215.6 5.2 collective-permute-start.3
  221.1 10.0 collective-permute-start.4
  222.8 8.3 collective-permute-start.5
  235.8 4.9 collective-permute-start.1
  241.0 5.2 collective-permute-start.3
  246.5 10.4 %collective-permute-start.4 = (f32[20,36,2]{2,1,0:T(8,128)S(1)}, f32[20,36,2]{2,1,0:T(8,128)S(1)}, u32[]{:S(2)}, u32[]{:S(2)}) collective-permute-start(f32[20,36,2]{2,1,0:T(8,128)S(1)} %get-tuple-element.403), channel_id=1, source_target_pairs={{0,1},{1,2},{2,3},{3,0},{4,5},{5,6},{6,7},{7,4},{8,9},{9,10},{10,1... | collective-permute-start | bytes 17288 | tf_op jit(solution)/shard_map/while/body/eval_jaxpr/ppermute | solution.py:18
  247.9 9.0 collective-permute-start.5
  261.5 4.9 collective-permute-start.1
  266.8 5.2 collective-permute-start.3
  272.3 9.9 collective-permute-start.4
  273.6 8.6 collective-permute-start.5
  286.9 4.9 collective-permute-start.1
  292.2 5.2 collective-permute-start.3
  297.7 9.2 collective-permute-start.4
  299.0 8.0 collective-permute-start.5
  311.7 4.9 collective-permute-start.1
  317.0 5.2 collective-permute-start.3
  322.5 9.8 collective-permute-start.4
  324.1 8.2 collective-permute-start.5
  337.0 4.9 collective-permute-start.1
  342.2 5.2 collective-permute-start.3
  347.7 10.4 %collective-permute-start.4 = (f32[20,36,2]{2,1,0:T(8,128)S(1)}, f32[20,36,2]{2,1,0:T(8,128)S(1)}, u32[]{:S(2)}, u32[]{:S(2)}) collective-permute-start(f32[20,36,2]{2,1,0:T(8,128)S(1)} %get-tuple-element.403), channel_id=1, source_target_pairs={{0,1},{1,2},{2,3},{3,0},{4,5},{5,6},{6,7},{7,4},{8,9},{9,10},{10,1... | collective-permute-start | bytes 17288 | tf_op jit(solution)/shard_map/while/body/eval_jaxpr/ppermute | solution.py:18
  349.1 9.0 collective-permute-start.5
  362.7 4.9 collective-permute-start.1
  368.0 5.2 collective-permute-start.3
  373.5 9.9 collective-permute-start.4
  374.8 8.6 collective-permute-start.5
  388.1 4.9 collective-permute-start.1
  393.4 5.2 collective-permute-start.3
  398.9 9.2 collective-permute-start.4
  400.2 8.0 collective-permute-start.5
  (33 other events, 126.2 us)
